TPU v7x, 128 devices: a whole 4x4x4 slice. The times are simulated.
128 devices in a mesh: wide: 8 (over z_hi, y), narrow: 16 (over x, z_lo, core).
Axes of the slice: x: 4, y: 4, z: 4 (z_hi: 2, z_lo: 2; z = z_hi * 2 + z_lo), core: 2. Of those that a mesh axis runs over, the one named last changes fastest.
Arguments:
- hinv_start: float32 [16384, 16384], P('wide', 'narrow'), as said below
- weights: bfloat16 [2048, 16384], P('narrow', 'wide'), may hold values from -6 to 6
- removed: int32 [1, 512], replicated, may hold values from 0 to 16383, as said below
Outputs:
- hinv_out: float32 [16384, 16384], P('wide', 'narrow')
- weights_out: bfloat16 [2048, 16384], P('narrow', 'wide')
Inputs may be any that keep to these rules, and one draw needn't show every extreme that they name: `removed`: all 1 x 512 indices are distinct; 0 and 16383 are always among them. `hinv_start`: symmetric and positive definite.
All inputs are finite; a program needn't handle non-finite values. Where the computation divides by a largest or mean magnitude, that divisor is 1e-20 or more.
Results may differ from a plain program's by a relative error of at most 0.0036.
Values may be sent and summed in bfloat16 or wider, within the bound.
No kernel may reach another device: no remote copies, remote signals or barrier semaphores. Data moves between devices by JAX's collectives and lax.ppermute only.
A program may use at most 128 MiB of HBM per device.

v0:
```python
import jax
import jax.numpy as jnp
from jax import lax
from jax.sharding import PartitionSpec as P

ITERS = 8


def from_root(x, axis, root):
    mine = lax.axis_index(axis) == root
    return lax.psum(jnp.where(mine, x, jnp.zeros_like(x)), axis)


def per_device(hinv_start, weights, removed):
    wide_count = lax.axis_size("wide")
    narrow_count = lax.axis_size("narrow")
    row_count, col_count = hinv_start.shape
    row_start = lax.axis_index("wide") * row_count
    col_start = lax.axis_index("narrow") * col_count
    blocks_each = narrow_count // wide_count
    block = removed.shape[1]
    identity = jnp.eye(block, dtype=jnp.float32)
    hess = hinv_start
    wmat = weights
    column_ids = row_start + jnp.arange(row_count, dtype=jnp.int32)
    picked = removed[0]
    row_hit = (picked >= row_start) & (picked < row_start + row_count)
    row_local = jnp.clip(picked - row_start, 0, row_count - 1)
    col_hit = (picked >= col_start) & (picked < col_start + col_count)
    col_local = jnp.clip(picked - col_start, 0, col_count - 1)
    row_part = jnp.where(row_hit[:, None], jnp.take(hess, row_local, axis=0), 0.0)
    weight_part = jnp.where(
        row_hit[None, :], jnp.take(wmat, row_local, axis=1).astype(jnp.float32), 0.0
    )
    rows_here, chosen = lax.psum((row_part, weight_part), "wide")
    pivot_part = jnp.where(col_hit[None, :], jnp.take(rows_here, col_local, axis=1), 0.0)
    pivot = lax.psum(pivot_part, "narrow")
    first_root = lax.axis_index("wide") * blocks_each
    col_part = jnp.where(col_hit[None, :], jnp.take(hess, col_local, axis=1), 0.0)
    columns = lax.psum(col_part, "narrow")
    rounded = rows_here.astype(jnp.bfloat16)
    pieces = []
    for offset in range(blocks_each):
        pieces.append(from_root(rounded, "narrow", first_root + offset))
    panel = jnp.concatenate(pieces, axis=1)
    scale = 1.0 / jnp.max(jnp.sum(jnp.abs(pivot), axis=1))
    start_guess = identity * scale
    width = block // wide_count
    own = lax.axis_index("wide") * width
    eye_cols = lax.dynamic_slice_in_dim(identity, own, width, 1)
    current = lax.dynamic_slice_in_dim(start_guess, own, width, 1)
    for turn in range(ITERS):
        right = 2.0 * eye_cols - jnp.dot(pivot, current, precision=lax.Precision.HIGHEST)

        def add_wide(total, piece, start, right=right):
            return jnp.dot(piece, right, precision=lax.Precision.HIGHEST)

        current = add_wide(
            jnp.zeros((block, width), jnp.float32),
            lax.all_gather(current, "wide", axis=1, tiled=True),
            jnp.int32(0),
        )
    inverse = lax.all_gather(current, "wide", axis=1, tiled=True)
    gain = jnp.dot(chosen, inverse, precision=lax.Precision.HIGHEST).astype(jnp.bfloat16)
    delta = jnp.dot(gain, panel, preferred_element_type=jnp.float32)
    cleared = jnp.any(picked[:, None] == column_ids[None, :], axis=0)
    wmat = jnp.where(cleared[None, :], 0.0, wmat.astype(jnp.float32) - delta).astype(jnp.bfloat16)
    inner_rows = jnp.dot(inverse, rows_here, precision=lax.Precision.HIGHEST)
    hess = hess - jnp.dot(columns, inner_rows, precision=lax.Precision.HIGHEST)
    return (hess, wmat)


def solution(mesh):
    return jax.shard_map(
        per_device,
        mesh=mesh,
        in_specs=(P("wide", "narrow"), P("narrow", "wide"), P()),
        out_specs=(P("wide", "narrow"), P("narrow", "wide")),
        check_vma=False,
    )
```

profile of v0, /device:TPU:0, one launch (start us, length us, event | category | flops | bytes accessed | tf_op | source)
XLA Modules:
  0.0 836.0 jit_solution(4168252360116877082)
XLA Ops:
  12.0 6.2 gather_fusion.1
  20.9 9.1 %copy.15 = f32[2048,1024]{0,1:T(8,128)} copy(f32[2048,1024]{1,0:T(8,128)} %param.3) | data formatting | bytes 16777216 | tf_op args[0]
  30.0 9.0 %gather_fusion = f32[512,2048]{1,0:T(8,128)} fusion(f32[2048,1024]{0,1:T(8,128)} %copy.15, s32[1024]{0:T(1024)S(1)} %pad_clamp_fusion.1), kind=kCustom, calls=%fused_computation | custom fusion | bytes 8390656 | tf_op jit(solution)/shard_map/jit(_take)/gather | solution.py:39
  39.0 4.7 select_bitcast_fusion
  43.7 73.7 %all-reduce.9.cloned.1.call-done = (f32[512,1024]{1,0:T(8,128)}, f32[128,512]{0,1:T(8,128)}) async-done(((f32[512,1024]{1,0:T(8,128)}, f32[128,512]{0,1:T(8,128)}), (f32[512,1024]{1,0:T(8,128)}, f32[128,512]{0,1:T(8,128)})) %all-reduce.9.cloned.1.call-update) | async-done | bytes 2359312 | tf_op jit(solution)/shard_map/psum | solution.py:35
  122.7 135.8 %all-reduce.7.cloned.1.call-done = (f32[2048,512]{0,1:T(8,128)}, f32[512,512]{1,0:T(8,128)}) async-done(((f32[2048,512]{0,1:T(8,128)}, f32[512,512]{1,0:T(8,128)}), (f32[2048,512]{0,1:T(8,128)}, f32[512,512]{1,0:T(8,128)})) %all-reduce.7.cloned.1.call-update) | async-done | bytes 5242896 | tf_op jit(solution)/shard_map/psum | solution.py:40
  262.0 2.4 convolution_subtract_fusion.9
  264.4 45.5 %all-gather.10.cloned.1.call-done = f32[512,512]{0,1:T(8,128)} async-done(((f32[512,64]{0,1:T(8,128)}), f32[512,512]{0,1:T(8,128)}) %all-gather.10.cloned.1.call-update) | async-done | bytes 1048592 | tf_op jit(solution)/shard_map/all_gather | solution.py:60
  309.9 2.7 fusion.7
  312.7 2.1 convolution_subtract_fusion.8
  314.7 44.0 %all-gather.12.cloned.1.call-done = f32[512,512]{0,1:T(8,128)} async-done(((f32[512,64]{0,1:T(8,128)}), f32[512,512]{0,1:T(8,128)}) %all-gather.12.cloned.1.call-update) | async-done | bytes 1048592 | tf_op jit(solution)/shard_map/all_gather | solution.py:60
  358.7 2.7 fusion.8
  363.5 44.0 %all-gather.14.cloned.1.call-done = f32[512,512]{0,1:T(8,128)} async-done(((f32[512,64]{0,1:T(8,128)}), f32[512,512]{0,1:T(8,128)}) %all-gather.14.cloned.1.call-update) | async-done | bytes 1048592 | tf_op jit(solution)/shard_map/all_gather | solution.py:60
  407.5 2.7 fusion.9
  410.4 2.1 convolution_subtract_fusion.6
  412.4 43.8 %all-gather.16.cloned.1.call-done = f32[512,512]{0,1:T(8,128)} async-done(((f32[512,64]{0,1:T(8,128)}), f32[512,512]{0,1:T(8,128)}) %all-gather.16.cloned.1.call-update) | async-done | bytes 1048592 | tf_op jit(solution)/shard_map/all_gather | solution.py:60
  456.3 2.7 fusion.10
  461.1 44.1 %all-gather.18.cloned.1.call-done = f32[512,512]{0,1:T(8,128)} async-done(((f32[512,64]{0,1:T(8,128)}), f32[512,512]{0,1:T(8,128)}) %all-gather.18.cloned.1.call-update) | async-done | bytes 1048592 | tf_op jit(solution)/shard_map/all_gather | solution.py:60
  505.1 2.7 fusion.11
  507.9 2.2 convolution_subtract_fusion.4
  510.1 43.9 %all-gather.20.cloned.1.call-done = f32[512,512]{0,1:T(8,128)} async-done(((f32[512,64]{0,1:T(8,128)}), f32[512,512]{0,1:T(8,128)}) %all-gather.20.cloned.1.call-update) | async-done | bytes 1048592 | tf_op jit(solution)/shard_map/all_gather | solution.py:60
  554.0 2.7 fusion.12
  558.8 44.1 %all-gather.22.cloned.1.call-done = f32[512,512]{0,1:T(8,128)} async-done(((f32[512,64]{0,1:T(8,128)}), f32[512,512]{0,1:T(8,128)}) %all-gather.22.cloned.1.call-update) | async-done | bytes 1048592 | tf_op jit(solution)/shard_map/all_gather | solution.py:60
  602.9 2.7 fusion.13
  607.7 44.0 %all-gather.24.cloned.1.call-done = f32[512,512]{0,1:T(8,128)} async-done(((f32[512,64]{0,1:T(8,128)}), f32[512,512]{0,1:T(8,128)}) %all-gather.24.cloned.1.call-update) | async-done | bytes 1048592 | tf_op jit(solution)/shard_map/all_gather | solution.py:60
  651.7 2.7 fusion.14
  656.9 43.7 %all-gather.26.cloned.1.call-done = f32[512,512]{0,1:T(8,128)} async-done(((f32[512,64]{0,1:T(8,128)}), f32[512,512]{0,1:T(8,128)}) %all-gather.26.cloned.1.call-update) | async-done | bytes 1048592 | tf_op jit(solution)/shard_map/all_gather | solution.py:63
  700.6 2.6 convolution_convert_fusion
  703.2 4.7 fusion.15
  708.0 17.1 %convolution_subtract_fusion = f32[2048,1024]{1,0:T(8,128)} fusion(f32[2048,1024]{1,0:T(8,128)} %param.3, f32[2048,512]{0,1:T(8,128)S(1)} %copy-done.2, f32[512,1024]{1,0:T(8,128)S(1)} %fusion.15), kind=kOutput, calls=%fused_computation.6 | convolution fusion | flops 12886999040 | bytes 23068672 | tf_op jit(solution)/shard_map/dot_general | solution.py:69
  725.0 101.4 %all-reduce.11.cloned.1.call-done = (bf16[512,1024]{1,0:T(8,128)(2,1)}, bf16[512,1024]{1,0:T(8,128)(2,1)}) async-done(((bf16[512,1024]{1,0:T(8,128)(2,1)}, bf16[512,1024]{1,0:T(8,128)(2,1)}), (bf16[512,1024]{1,0:T(8,128)(2,1)}, bf16[512,1024]{1,0:T(8,128)(2,1)})) %all-reduce.11.cloned.1.call-update) | async-done | bytes 2097168 | tf_op jit(solution)/shard_map/psum | solution.py:11
  826.4 2.8 fusion.1
  (60 shorter events, 26.8 us)
Async XLA Ops:
  7.2 110.2 %all-reduce.9.cloned.1.call-start = ((), (), s32[]{:S(2)}) async-start(), calls=%async_computation.10 | async-start | bytes 4718592 | tf_op jit(solution)/shard_map/psum | solution.py:35
  20.8 237.7 %all-reduce.7.cloned.1.call-start = ((), (), s32[]{:S(2)}) async-start(), calls=%async_computation.9 | async-start | bytes 10485760 | tf_op jit(solution)/shard_map/psum | solution.py:40
  122.5 187.4 %all-gather.10.cloned.1.call-start = ((), (), s32[]{:S(2)}) async-start(), calls=%async_computation | async-start | bytes 1179648 | tf_op jit(solution)/shard_map/all_gather | solution.py:60
  258.5 54.2 %copy-start = (f32[512,512]{1,0:T(8,128)S(1)}, f32[512,512]{1,0:T(8,128)}, u32[]{:S(2)}) copy-start(f32[512,512]{1,0:T(8,128)} %get-tuple-element.5) | copy-start | bytes 3145732
  262.0 96.7 %all-gather.12.cloned.1.call-start = ((), (), s32[]{:S(2)}) async-start(), calls=%async_computation.1 | async-start | bytes 1179648 | tf_op jit(solution)/shard_map/all_gather | solution.py:60
  312.6 94.9 %all-gather.14.cloned.1.call-start = ((), (), s32[]{:S(2)}) async-start(), calls=%async_computation.2 | async-start | bytes 1179648 | tf_op jit(solution)/shard_map/all_gather | solution.py:60
  361.4 94.9 %all-gather.16.cloned.1.call-start = ((), (), s32[]{:S(2)}) async-start(), calls=%async_computation.3 | async-start | bytes 1179648 | tf_op jit(solution)/shard_map/all_gather | solution.py:60
  410.2 95.0 %all-gather.18.cloned.1.call-start = ((), (), s32[]{:S(2)}) async-start(), calls=%async_computation.4 | async-start | bytes 1179648 | tf_op jit(solution)/shard_map/all_gather | solution.py:60
  458.9 95.1 %all-gather.20.cloned.1.call-start = ((), (), s32[]{:S(2)}) async-start(), calls=%async_computation.5 | async-start | bytes 1179648 | tf_op jit(solution)/shard_map/all_gather | solution.py:60
  507.8 146.8 %copy-start.1 = (f32[512,1024]{1,0:T(8,128)S(1)}, f32[512,1024]{1,0:T(8,128)}, u32[]{:S(2)}) copy-start(f32[512,1024]{1,0:T(8,128)} %get-tuple-element.6) | copy-start | bytes 6291460
  507.8 95.1 %all-gather.22.cloned.1.call-start = ((), (), s32[]{:S(2)}) async-start(), calls=%async_computation.6 | async-start | bytes 1179648 | tf_op jit(solution)/shard_map/all_gather | solution.py:60
  556.7 95.0 %all-gather.24.cloned.1.call-start = ((), (), s32[]{:S(2)}) async-start(), calls=%async_computation.7 | async-start | bytes 1179648 | tf_op jit(solution)/shard_map/all_gather | solution.py:60
  605.6 95.0 %all-gather.26.cloned.1.call-start = ((), (), s32[]{:S(2)}) async-start(), calls=%async_computation.8 | async-start | bytes 1179648 | tf_op jit(solution)/shard_map/all_gather | solution.py:63
  607.7 48.6 %copy-start.5 = (s32[1,512]{1,0:T(1,128)S(1)}, s32[1,512]{1,0:T(1,128)}, u32[]{:S(2)}) copy-start(s32[1,512]{1,0:T(1,128)} %param.5) | copy-start | bytes 6148
  607.7 92.9 %copy-start.4 = (f32[128,512]{0,1:T(8,128)S(1)}, f32[128,512]{0,1:T(8,128)}, u32[]{:S(2)}) copy-start(f32[128,512]{0,1:T(8,128)} %get-tuple-element.7) | copy-start | bytes 786436
  654.4 172.0 %all-reduce.11.cloned.1.call-start = ((), (), s32[]{:S(2)}) async-start(), calls=%async_computation.11 | async-start | bytes 4194304 | tf_op jit(solution)/shard_map/psum | solution.py:11
  700.6 7.3 copy-start.2
  707.9 118.4 %copy-start.3 = (bf16[128,2048]{1,0:T(8,128)(2,1)S(1)}, bf16[128,2048]{1,0:T(8,128)(2,1)}, u32[]{:S(2)}) copy-start(bf16[128,2048]{1,0:T(8,128)(2,1)} %param.4) | copy-start | bytes 1572868
Sparse Core Ops, SparseCore 0:
  21.0 96.3 all-reduce.8
  122.7 135.7 all-reduce.6
  262.1 47.7 all-gather.9
  312.7 45.9 all-gather.11
  361.5 45.9 all-gather.13
  410.3 45.9 all-gather.15
  459.2 45.9 all-gather.17
  508.1 45.9 all-gather.19
  556.9 45.9 all-gather.21
  605.7 45.9 all-gather.23
  654.6 45.9 all-gather.25
  703.0 123.3 all-reduce.10
where the time goes:
time: 837 us; the launch traced here: 836 us
  waiting for transfers between devices  708 us (85%)
  matrix products  65.4 us (8%)
  local copies, waits for them, and re-layouts  30.9 us (4%)
  other arithmetic  15.7 us (2%)
  between operations  15.1 us (2%)
    all_gather x8, waiting for transfers between devices, per_device(): lax.all_gather(current, 'wide', axis=1, tiled=True)  353 us
    psum x1, waiting for transfers between devices, per_device(): columns = lax.psum(col_part, 'narrow')  136 us
    psum x1, waiting for transfers between devices, from_root(): return lax.psum(jnp.where(mine, x, jnp.zeros_like(x)), axis)  101 us
    psum x1, waiting for transfers between devices, per_device(): rows_here, chosen = lax.psum((row_part, weight_part), 'wide')  73.7 us
    all_gather x1, waiting for transfers between devices, per_device(): inverse = lax.all_gather(current, 'wide', axis=1, tiled=True)  43.7 us
    dot_general x8, matrix products, add_wide(): return jnp.dot(piece, right, precision=lax.Precision.HIGHEST)  21.3 us
    dot_general x1, matrix products, per_device(): hess = hess - jnp.dot(columns, inner_rows, precision=lax.Precision.HIGHEST)  17.1 us
    dot_general x8, matrix products, per_device(): jnp.dot(pivot, current, precision=lax.Precision.HIGHEST)  16.9 us
  transfers between devices with their start and end apart: 12, of which 12 were waited for; matrix products, arithmetic and copies ran while one was open for 8% of the time, Pallas kernels for 0%

commit v1 on v0

v1 whole, which is shorter than its diff:
```python
import functools

import jax
import jax.numpy as jnp
from jax import lax
from jax.experimental import pallas as pl
from jax.experimental.pallas import tpu as pltpu
from jax.sharding import PartitionSpec as P


ITERS = 8
ROOM = 96
F32 = jnp.float32
BF16 = jnp.bfloat16
I32 = jnp.int32
BOTH = ("wide", "narrow")
VMEM = pltpu.MemorySpace.VMEM
SMEM = pltpu.MemorySpace.SMEM


def hop(a, axis, size, move):
    return lax.ppermute(a, axis, [(i, move(i)) for i in range(size)])


def z_hi_swap(a):
    return hop(a, "wide", 8, lambda i: (i + 4) % 8)


def y_step(a, k):
    return hop(a, "wide", 8, lambda i: (i // 4) * 4 + (i + k) % 4)


def core_swap(a):
    return hop(a, "narrow", 16, lambda i: i ^ 1)


def z_lo_swap(a):
    return hop(a, "narrow", 16, lambda i: i ^ 2)


def x_step(a, k):
    return hop(a, "narrow", 16, lambda i: (i + 4 * k) % 16)


def limit(mib):
    return pltpu.CompilerParams(vmem_limit_bytes=mib * 2**20)


def cost(flops, size):
    return pl.CostEstimate(flops=flops, bytes_accessed=size, transcendentals=0)


def split(a):
    hi = a.astype(BF16)
    return hi, (a - hi.astype(F32)).astype(BF16)


def split3(a):
    hi = a.astype(BF16)
    rest = a - hi.astype(F32)
    mid = rest.astype(BF16)
    return hi, mid, (rest - mid.astype(F32)).astype(BF16)


def dot(a, b):
    return jnp.dot(a, b, preferred_element_type=F32)


def exact_dot(a, hot):
    hi, mid, low = split3(a)
    return (dot(hi, hot) + dot(mid, hot)) + dot(low, hot)


def times(left, right):
    (lh, ll), (rh, rl) = left, right
    return dot(lh, rh) + (dot(lh, rl) + dot(ll, rh))


def hot_rows(count, lanes_index):
    ids = lax.broadcasted_iota(I32, (count, lanes_index.shape[1]), 0)
    return (ids == lanes_index).astype(BF16)


def pick_kernel(index_smem, index_vec, hess, wmat, packed, plain, pivot, rows, chosen, wpack, wbuf, owned, sem, wsem):
    block = index_vec.shape[1]
    local_rows, local_cols = hess.shape
    row_start = lax.axis_index("wide") * local_rows
    col_start = lax.axis_index("narrow") * local_cols
    wcopy = pltpu.make_async_copy(wmat, wbuf, wsem)
    wcopy.start()

    def find(i, count):
        owned[count] = i
        r = index_smem[0, i] - row_start
        return count + jnp.where((r >= 0) & (r < local_rows), 1, 0)

    count = jnp.minimum(lax.fori_loop(0, block, find, 0, unroll=16), ROOM)

    def row_of(k):
        return index_smem[0, owned[k]] - row_start

    def row_copy(k):
        return pltpu.make_async_copy(hess.at[pl.ds(row_of(k), 1), :], rows.at[pl.ds(k, 1), :], sem)

    def fetch(k, carry):
        row_copy(k).start()
        return carry

    rows[...] = jnp.zeros_like(rows)
    lax.fori_loop(0, count, fetch, 0)
    wpack[...] = jnp.zeros_like(wpack)
    hot_w = hot_rows(wmat.shape[1], index_vec[...] - row_start)
    wcopy.wait()
    chosen[...] = dot(wbuf[...], hot_w).T
    hot_c = hot_rows(local_cols, index_vec[...] - col_start)

    def settle(k, carry):
        row_copy(k).wait()
        return carry

    def place(k, carry):
        wpack[pl.ds(k, 1), :] = chosen[pl.ds(owned[k], 1), :]
        return carry

    lax.fori_loop(0, count, place, 0)
    lax.fori_loop(0, count, settle, 0)
    found = exact_dot(rows[...], hot_c)
    short = rows[:ROOM, :].astype(BF16)
    packed[:, :local_cols] = short
    plain[...] = short
    packed[:, local_cols:] = wpack[:ROOM, :].astype(BF16)
    turned = found.T
    for d in range(128):
        pivot[d] = turned[d * 4 : (d + 1) * 4, :]


def pick(hess, wmat, removed):
    block = removed.shape[1]
    cols = hess.shape[1]
    return pl.pallas_call(
        pick_kernel,
        in_specs=[
            pl.BlockSpec(memory_space=SMEM),
            pl.BlockSpec(memory_space=VMEM),
            pl.BlockSpec(memory_space=pl.ANY),
            pl.BlockSpec(memory_space=pl.ANY),
        ],
        out_specs=[pl.BlockSpec(memory_space=VMEM)] * 3,
        out_shape=[
            jax.ShapeDtypeStruct((ROOM, cols + 128), BF16),
            jax.ShapeDtypeStruct((ROOM, cols), BF16),
            jax.ShapeDtypeStruct((128, block // 128, 128), F32),
        ],
        scratch_shapes=[
            pltpu.VMEM((128, cols), F32),
            pltpu.VMEM((block, 128), F32),
            pltpu.VMEM((128, 128), F32),
            pltpu.VMEM(wmat.shape, wmat.dtype),
            pltpu.SMEM((block + 1,), I32),
            pltpu.SemaphoreType.DMA,
            pltpu.SemaphoreType.DMA,
        ],
        compiler_params=pltpu.CompilerParams(vmem_limit_bytes=67043328),
        name="pick",
    )(removed, removed, hess, wmat)


def group_of(index, size):
    return sum((index >= w * size).astype(I32) for w in range(1, 8))


def middle_kernel(index, parts, out, slot, *, size):
    block = index.shape[1]
    group = group_of(index[...], size).astype(F32)
    turned = jnp.broadcast_to(group, (8, block)).T[:, :1]
    first = lax.broadcasted_iota(I32, (block, block), 0)
    second = lax.broadcasted_iota(I32, (block, block), 1)
    same = turned == group
    before = jnp.sum((same & (first < second)).astype(F32), axis=0, keepdims=True)
    lane = (group * 128.0 + before).astype(I32)
    ahead = jnp.sum((same & (second < first)).astype(F32), axis=1, keepdims=True)
    slot[...] = (turned * float(ROOM) + ahead).astype(I32)
    lanes = []
    for w in range(8):
        total = parts[w * 16]
        for n in range(1, 16):
            total = total + parts[w * 16 + n]
        lanes.append(total)
    packed = jnp.concatenate(lanes, axis=1)
    rows = exact_dot(packed, hot_rows(8 * 128, lane))
    for d in range(128):
        out[d] = rows


def middle(index, parts, size):
    block = index.shape[1]
    return pl.pallas_call(
        functools.partial(middle_kernel, size=size),
        in_specs=[pl.BlockSpec(memory_space=VMEM)] * 2,
        out_specs=[pl.BlockSpec(memory_space=VMEM)] * 2,
        out_shape=[
            jax.ShapeDtypeStruct((128, block // 128, block), F32),
            jax.ShapeDtypeStruct((block, 1), I32),
        ],
        compiler_params=limit(16),
        name="middle",
    )(index, parts)


def inverse_kernel(tiles, out, full):
    block = full.shape[0]
    each = block // 128
    for d in range(128):
        full[d * each : (d + 1) * each, :] = tiles[d]
    a = full[...]
    total = jnp.sum(jnp.abs(a), axis=0, keepdims=True)
    scale = 1.0 / jnp.max(total)
    shape = (block, block)
    eye = (lax.broadcasted_iota(I32, shape, 0) == lax.broadcasted_iota(I32, shape, 1)).astype(F32)
    e = eye - a * scale
    p = (eye + e) * scale
    es = split(e)
    e = times(es, es)
    for turn in range(1, ITERS):
        es = split(e)
        if turn < ITERS - 1:
            e = times(es, es)
        p = p + times(split(p), es)
    out[...] = p


def inverse_of(tiles):
    block = tiles.shape[2]
    return pl.pallas_call(
        inverse_kernel,
        in_specs=[pl.BlockSpec(memory_space=VMEM)],
        out_specs=pl.BlockSpec(memory_space=VMEM),
        out_shape=jax.ShapeDtypeStruct((block, block), F32),
        scratch_shapes=[pltpu.VMEM((block, block), F32)],
        compiler_params=limit(16),
        cost_estimate=cost(14 * 3 * 2 * block**3, 8 * block**2),
        name="inverse",
    )(tiles)


def arrange_kernel(tab, slot, s0, s1, s2, s3, s4, s5, out, stack):
    at = lambda i: pl.ds(pl.multiple_of(tab[i] * ROOM, 16), ROOM)
    for i, part in enumerate((s0[...], s1[...], s2[0], s2[1], s3[0], s3[1], s4[...], s5[...])):
        stack[at(i), :] = part
    ids = lax.broadcasted_iota(I32, (slot.shape[0], 8 * ROOM), 1)
    hot = (ids == slot[...]).astype(BF16)
    cols = out.shape[1]
    for c in range(0, cols, 256):
        d = min(c + 256, cols)
        out[:, c:d] = dot(hot, stack[:, c:d]).astype(BF16)


def arrange(table, slot, groups):
    block = slot.shape[0]
    cols = groups[0].shape[-1]
    return pl.pallas_call(
        arrange_kernel,
        in_specs=[pl.BlockSpec(memory_space=SMEM)] + [pl.BlockSpec(memory_space=VMEM)] * 7,
        out_specs=pl.BlockSpec(memory_space=VMEM),
        out_shape=jax.ShapeDtypeStruct((block, cols), BF16),
        scratch_shapes=[pltpu.VMEM((8 * ROOM, cols), BF16)],
        compiler_params=limit(16),
        cost_estimate=cost(2 * block * 8 * ROOM * cols, 4 * block * cols),
    )(table, slot, *groups)


def finish_kernel(tab, index, inv, rows, mine, other, hess, wmat, hess_out, wmat_out,
                  held, both, wheld, wnew, sem_in, sem_out, sem_w):
    block = inv.shape[0]
    size, cols = hess.shape
    step = size // 8
    at = lambda t: pl.ds(pl.multiple_of(tab[t] * step, step), step)
    wcopy = pltpu.make_async_copy(wmat, wheld, sem_w.at[0])
    wcopy.start()
    loads = [pltpu.make_async_copy(hess.at[at(t), :], held.at[t], sem_in.at[t]) for t in range(8)]
    for load in loads:
        load.start()
    x_hi, x_lo = split(inv[...])
    for c in range(0, cols, 256):
        r = rows[:, c : c + 256]
        both[:, c : c + 256] = (dot(x_hi, r) + dot(x_lo, r)).astype(BF16)
    chosen = rows[:, cols:].T
    gain = (dot(chosen, x_hi) + dot(chosen, x_lo)).astype(BF16)
    picked = jnp.broadcast_to(index[...].astype(F32), (8, block)).T[:, :1].astype(I32)
    row_start = lax.axis_index("wide") * size
    wcopy.wait()
    stores = []
    for t in range(8):
        left = mine if t < 4 else other
        panel = left[:, (t % 4) * step : (t % 4 + 1) * step]
        turned = panel.T
        loads[t].wait()
        for c in range(0, cols, 512):
            held[t, :, c : c + 512] = held[t, :, c : c + 512] - dot(turned, both[:, c : c + 512])
        store = pltpu.make_async_copy(held.at[t], hess_out.at[at(t), :], sem_out.at[t])
        store.start()
        stores.append(store)
        ids = lax.broadcasted_iota(I32, (1, step), 1) + (row_start + tab[t] * step)
        hit = jnp.max((picked == ids).astype(F32), axis=0, keepdims=True)
        new = wheld[:, at(t)].astype(F32) - dot(gain, panel)
        wnew[:, at(t)] = jnp.where(hit > 0, 0.0, new).astype(BF16)
    last = pltpu.make_async_copy(wnew, wmat_out, sem_w.at[1])
    last.start()
    for store in stores:
        store.wait()
    last.wait()


def finish(order, index, inv, rows, mine, other, hess, wmat):
    block = inv.shape[0]
    size, cols = hess.shape
    vmem = pl.BlockSpec(memory_space=VMEM)
    anywhere = pl.BlockSpec(memory_space=pl.ANY)
    return pl.pallas_call(
        finish_kernel,
        in_specs=[pl.BlockSpec(memory_space=SMEM)] + [vmem] * 5 + [anywhere] * 2,
        out_specs=[anywhere] * 2,
        out_shape=[jax.ShapeDtypeStruct(hess.shape, F32), jax.ShapeDtypeStruct(wmat.shape, BF16)],
        scratch_shapes=[
            pltpu.VMEM((8, size // 8, cols), F32),
            pltpu.VMEM((block, cols), BF16),
            pltpu.VMEM(wmat.shape, BF16),
            pltpu.VMEM(wmat.shape, BF16),
            pltpu.SemaphoreType.DMA((8,)),
            pltpu.SemaphoreType.DMA((8,)),
            pltpu.SemaphoreType.DMA((2,)),
        ],
        compiler_params=limit(56),
        cost_estimate=cost(size * cols * block * 2, size * cols * 8),
        name="finish",
    )(order, index, inv, rows, mine, other, hess, wmat)


def ring_sum(a, axis):
    size = lax.axis_size(axis)

    def turn(k, carry):
        total, moving = carry
        moving = hop(moving, axis, size, lambda i: (i + 1) % size)
        return total + moving, moving

    return lax.fori_loop(0, size - 1, turn, (a, a))[0]


def masked_take(src, index, start, axis):
    size = src.shape[axis]
    shape = list(src.shape)
    shape[axis] = index.shape[0]

    def one(k, out):
        at = index[k] - start
        piece = lax.dynamic_slice_in_dim(src, jnp.clip(at, 0, size - 1), 1, axis)
        piece = jnp.where((at >= 0) & (at < size), piece.astype(F32), 0.0)
        return lax.dynamic_update_slice_in_dim(out, piece, k, axis)

    return lax.fori_loop(0, index.shape[0], one, jnp.zeros(shape, F32))


def general_gather(hess, wmat, removed, core):
    row_count, col_count = hess.shape
    row_start = lax.axis_index("wide") * row_count
    col_start = lax.axis_index("narrow") * col_count
    index = removed[0]
    block = index.shape[0]
    rows = ring_sum(masked_take(hess, index, row_start, 0), "wide")
    chosen = ring_sum(masked_take(wmat, index, row_start, 1), "wide")
    pivot = ring_sum(masked_take(rows, index, col_start, 1), "narrow")
    columns = ring_sum(masked_take(hess, index, col_start, 1), "narrow")
    half = row_count // 2
    mine = lax.dynamic_slice_in_dim(columns, core * half, half, 0).T.astype(BF16)
    panel = jnp.concatenate([rows, chosen.T], axis=1).astype(BF16)
    return pivot.reshape(128, block // 128, block), mine, panel


def packed_path(hess, wmat, removed):
    row_count, _ = hess.shape
    wide = lax.axis_index("wide")
    narrow = lax.axis_index("narrow")
    z_hi, y = wide // 4, wide % 4
    x, z_lo, core = narrow // 4, (narrow // 2) % 2, narrow % 2
    packed, plain, pivot = pick(hess, wmat, removed)

    parts = lax.all_to_all(pivot, BOTH, 0, 0)
    swap = []
    for w in range(8):
        for n in range(16):
            px, pz, pc = n // 4, (n // 2) % 2, n % 2
            tx, tz = (px + w // 2) % 4, pz ^ (w % 2)
            swap.append((w * 16 + n, (n // 2) * 16 + tx * 4 + tz * 2 + pc))
    col = lax.ppermute(plain, BOTH, swap)
    far = z_hi_swap(packed)
    spread, slot = middle(removed, parts, row_count)
    tiles = lax.all_to_all(spread, BOTH, 0, 0)

    mate = z_lo_swap(col)
    pair = jnp.stack([col, mate])
    ahead, behind = x_step(pair, 1), x_step(pair, -1)
    cols = [col, mate, ahead, behind, x_step(ahead[0], 1), x_step(behind[1], -1)]
    near = jnp.stack([packed, far])
    up, down = y_step(near, 1), y_step(near, -1)
    rows = [packed, far, up, down, y_step(up[0], 1), y_step(down[1], -1)]

    w_of, g_of = [], []
    for step in (0, -1, 1, 2):
        for flip in (0, 1):
            w_of.append(((z_hi + flip) % 2) * 4 + (y + step) % 4)
            g_of.append(((x + step - wide // 2) % 4) * 2 + (z_lo + flip + wide) % 2)
    mine = arrange(jnp.stack(g_of).astype(I32), slot, cols)
    panel = arrange(jnp.stack(w_of).astype(I32), slot, rows)
    group = group_of(removed, row_count)
    counts = jnp.sum((group == jnp.arange(8, dtype=I32)[:, None]).astype(I32), axis=1)
    crowded = jnp.max(counts) > ROOM

    def again(state):
        return (jnp.zeros((), bool),) + general_gather(hess, wmat, removed, core)

    _, tiles, mine, panel = lax.while_loop(lambda state: state[0], again, (crowded, tiles, mine, panel))
    other = core_swap(mine)
    inv = inverse_of(tiles)
    order = jnp.stack([(core ^ (t // 4)) * 4 + t % 4 for t in range(8)]).astype(I32)
    return finish(order, removed, inv, panel, mine, other, hess, wmat)


def solution(mesh):
    return jax.shard_map(
        packed_path,
        mesh=mesh,
        in_specs=(P("wide", "narrow"), P("narrow", "wide"), P()),
        out_specs=(P("wide", "narrow"), P("narrow", "wide")),
        check_vma=False,
    )
```

time: 837 us -> 118 us (0.14)
  waiting for transfers between devices: 708 us -> 26.5 us
  matrix products: 65.4 us -> 0 us
  Pallas kernels: 0 us -> 37.7 us
  starting transfers between devices: 0.9 us -> 38.5 us
  local copies, waits for them, and re-layouts: 30.9 us -> 8.39 us
  between operations: 15.1 us -> 1.81 us
  other arithmetic: 15.7 us -> 3.23 us
    all_gather x9 -> x0, waiting for transfers between devices: 397 us -> none  [the longest x8 353 us: per_device(): lax.all_gather(current, 'wide', axis=1, tiled=True)]
    psum x3 -> x0, waiting for transfers between devices: 311 us -> none  [the longest x1 136 us: per_device(): columns = lax.psum(col_part, 'narrow')]
    dot_general x20 -> x0, matrix products: 65.4 us -> none  [the longest x8 21.3 us: add_wide(): return jnp.dot(piece, right, precision=lax.Precision.HIGHEST)]
    pallas_call x0 -> x6, Pallas kernels: none -> 37.7 us  [the longest x1 13.5 us: inverse_of(): pl.pallas_call(inverse_kernel, in_specs=[pl.BlockSpec(memory_space=VMEM)]...]
    ppermute x0 -> x12, waiting for transfers between devices: none -> 21.2 us  [the longest x11 21.2 us: hop(): return lax.ppermute(a, axis, [(i, move(i)) for i in range(size)])]
    ppermute x0 -> x12, starting transfers between devices: none -> 20.3 us  [the longest x11 18.7 us: hop(): return lax.ppermute(a, axis, [(i, move(i)) for i in range(size)])]
    gather x5 -> x0, local copies, waits for them, and re-layouts: 18.5 us -> none  [the longest x1 8.99 us: per_device(): jnp.take(hess, col_local, axis=1)]
    all_to_all x0 -> x2, starting transfers between devices: none -> 18.2 us  [the longest x1 12.3 us: packed_path(): parts = lax.all_to_all(pivot, BOTH, 0, 0)]
  transfers between devices with their start and end apart: 12 -> 14, of which waited for: 12 -> 3; matrix products, arithmetic and copies ran while one was open for 8% -> 7% of each run, Pallas kernels for 0% -> 18%
where the time goes in v1:
time: 118 us; the launch traced here: 116 us
  starting transfers between devices  38.5 us (33%)
  Pallas kernels  37.7 us (32%)
  waiting for transfers between devices  26.5 us (22%)
  local copies, waits for them, and re-layouts  8.39 us (7%)
  other arithmetic  3.23 us (3%)
  between operations  1.81 us (2%)
    ppermute x11, waiting for transfers between devices, hop(): return lax.ppermute(a, axis, [(i, move(i)) for i in range(size)])  21.2 us
    ppermute x11, starting transfers between devices, hop(): return lax.ppermute(a, axis, [(i, move(i)) for i in range(size)])  18.7 us
    pallas_call x1, Pallas kernels, inverse_of(): pl.pallas_call(inverse_kernel, in_specs=[pl.BlockSpec(memory_space=VMEM)]...  13.5 us
    all_to_all x1, starting transfers between devices, packed_path(): parts = lax.all_to_all(pivot, BOTH, 0, 0)  12.3 us
    pallas_call x1, Pallas kernels, finish(): pl.pallas_call(finish_kernel, in_specs=[pl.BlockSpec(memory_space=SMEM)]...  10.1 us
    pallas_call x1, Pallas kernels, pick(): pl.pallas_call(pick_kernel, in_specs=[pl.BlockSpec(memory_space=SMEM), pl...  6.34 us
    all_to_all x1, starting transfers between devices, packed_path(): tiles = lax.all_to_all(spread, BOTH, 0, 0)  5.89 us
    all_to_all x1, waiting for transfers between devices, packed_path(): parts = lax.all_to_all(pivot, BOTH, 0, 0)  5.3 us
  transfers between devices with their start and end apart: 14, of which 3 were waited for; matrix products, arithmetic and copies ran while one was open for 7% of the time, Pallas kernels for 18%

profile of v1, /device:TPU:0, one launch (start us, length us, event | category | flops | bytes accessed | tf_op | source)
XLA Modules:
  0.0 116.1 jit_solution(6027536811164903407)
XLA Ops:
  0.6 6.3 %pick.1 = (bf16[96,1152]{1,0:T(8,128)(2,1)}, bf16[96,1024]{1,0:T(8,128)(2,1)}, f32[128,4,128]{2,1,0:T(4,128)}) custom-call(s32[1,512]{1,0:T(1,128)} %index.3, s32[1,512]{1,0:T(1,128)} %index.3, f32[2048,1024]{1,0:T(8,128)} %hess.3, bf16[128,2048]{1,0:T(8,128)(2,1)} %wmat.3), custom_call_target="tpu_custom_call" | custom-call | tf_op jit(solution)/shard_map/pick/pallas_call | solution.py:140
  7.0 4.6 %collective-permute-start.10 = (bf16[96,1152]{1,0:T(8,128)(2,1)}, bf16[96,1152]{1,0:T(8,128)(2,1)S(1)}, u32[]{:S(2)}, u32[]{:S(2)}) collective-permute-start(bf16[96,1152]{1,0:T(8,128)(2,1)} %get-tuple-element.539.s0), channel_id=1, source_target_pairs={{0,64},{16,80},{32,96},{48,112},{64,0},{80,16},{96,32},{112,48},{1... | collective-permute-start | bytes 663560 | tf_op jit(solution)/shard_map/ppermute | solution.py:22
  11.5 1.6 %collective-permute-start.4 = (bf16[96,1024]{1,0:T(8,128)(2,1)}, bf16[96,1024]{1,0:T(8,128)(2,1)S(1)}, u32[]{:S(2)}, u32[]{:S(2)}) collective-permute-start(bf16[96,1024]{1,0:T(8,128)(2,1)} %get-tuple-element.538), channel_id=1, source_target_pairs={{0,0},{1,1},{2,18},{3,19},{4,36},{5,37},{6,54},{7,55},{8,72},{9,73... | collective-permute-start | bytes 589832 | tf_op jit(solution)/shard_map/ppermute | solution.py:395
  13.1 7.6 %collective-permute-done.10.s1 = bf16[96,1152]{1,0:T(8,128)(2,1)S(1)} collective-permute-done((bf16[96,1152]{1,0:T(8,128)(2,1)}, bf16[96,1152]{1,0:T(8,128)(2,1)S(1)}, u32[]{:S(2)}, u32[]{:S(2)}) %collective-permute-start.10) | collective-permute-done | bytes 221216 | tf_op jit(solution)/shard_map/ppermute | solution.py:22
  20.8 1.7 %pad_maximum_fusion.1 = bf16[2,96,1152]{2,1,0:T(8,128)(2,1)} fusion(bf16[1,96,1152]{2,1,0:T(8,128)(2,1)S(1)} %bitcast.56, bf16[1,96,1152]{2,1,0:T(8,128)(2,1)} %bitcast.55), kind=kLoop, calls=%fused_computation.8 | loop fusion | flops 221184 | bytes 884736 | tf_op jit(solution)/shard_map/stack | solution.py:404
  22.5 12.3 %all-to-all-start = ((f32[128,4,128]{2,1,0:T(4,128)}), f32[128,4,128]{2,1,0:T(4,128)S(1)}, u32[]{:S(2)}, u32[]{:S(2)}) async-start(f32[128,4,128]{2,1,0:T(4,128)} %get-tuple-element.535), calls=%async_computation | async-start | bytes 524288 | tf_op jit(solution)/shard_map/all_to_all | solution.py:388
  35.1 1.2 collective-permute-start.5
  36.2 0.7 fusion.6
  36.9 2.9 %collective-permute-start.12 = (bf16[2,96,1152]{2,1,0:T(8,128)(2,1)}, bf16[2,96,1152]{2,1,0:T(8,128)(2,1)S(1)}, u32[]{:S(2)}, u32[]{:S(2)}) collective-permute-start(bf16[2,96,1152]{2,1,0:T(8,128)(2,1)} %pad_maximum_fusion.1), channel_id=1, source_target_pairs={{0,48},{16,0},{32,16},{48,32},{64,112},{80,64},{96,80},{112,96},{1... | collective-permute-start | bytes 1327112 | tf_op jit(solution)/shard_map/ppermute | solution.py:22
  39.9 5.3 %all-to-all-done.parts = f32[128,4,128]{2,1,0:T(4,128)S(1)} async-done(((f32[128,4,128]{2,1,0:T(4,128)}), f32[128,4,128]{2,1,0:T(4,128)S(1)}, u32[]{:S(2)}, u32[]{:S(2)}) %all-to-all-start) | async-done | bytes 262176 | tf_op jit(solution)/shard_map/all_to_all | solution.py:388
  45.2 2.7 %middle.1 = (f32[128,4,512]{2,1,0:T(4,128)}, s32[512,1]{1,0:T(8,128)S(1)}) custom-call(s32[1,512]{1,0:T(1,128)} %index.3, f32[128,4,128]{2,1,0:T(4,128)S(1)} %all-to-all-done.parts), custom_call_target="tpu_custom_call" | custom-call | tf_op jit(solution)/shard_map/middle/pallas_call | solution.py:197
  47.9 5.9 %all-to-all-start.1 = ((f32[128,4,512]{2,1,0:T(4,128)}), f32[128,4,512]{2,1,0:T(4,128)}, u32[]{:S(2)}, u32[]{:S(2)}) async-start(f32[128,4,512]{2,1,0:T(4,128)} %get-tuple-element.536), calls=%async_computation.1 | async-start | bytes 2097152 | tf_op jit(solution)/shard_map/all_to_all | solution.py:398
  53.8 0.9 collective-permute-start.6
  54.7 2.4 %collective-permute-start.7 = (bf16[2,96,1024]{2,1,0:T(8,128)(2,1)S(1)}, bf16[2,96,1024]{2,1,0:T(8,128)(2,1)S(1)}, u32[]{:S(2)}, u32[]{:S(2)}) collective-permute-start(bf16[2,96,1024]{2,1,0:T(8,128)(2,1)S(1)} %pad_maximum_fusion.2), channel_id=1, source_target_pairs={{0,12},{1,13},{2,14},{3,15},{4,0},{5,1},{6,2},{7,3},{8,4},{9,5},{1... | collective-permute-start | bytes 1179656 | tf_op jit(solution)/shard_map/ppermute | solution.py:22
  57.1 0.7 slice_bitcast_fusion.1
  57.8 0.8 collective-permute-start.13
  58.7 0.7 slice_bitcast_fusion
  59.4 2.4 %collective-permute-start.14 = (bf16[96,1152]{1,0:T(8,128)(2,1)}, bf16[96,1152]{1,0:T(8,128)(2,1)S(1)}, u32[]{:S(2)}, u32[]{:S(2)}) collective-permute-start(bf16[96,1152]{1,0:T(8,128)(2,1)} %slice_bitcast_fusion), channel_id=1, source_target_pairs={{0,48},{16,0},{32,16},{48,32},{64,112},{80,64},{96,80},{112,96},{1... | collective-permute-start | bytes 663560 | tf_op jit(solution)/shard_map/ppermute | solution.py:22
  61.8 13.5 %collective-permute-done.6.s2 = bf16[2,96,1024]{2,1,0:T(8,128)(2,1)S(1)} collective-permute-done((bf16[2,96,1024]{2,1,0:T(8,128)(2,1)S(1)}, bf16[2,96,1024]{2,1,0:T(8,128)(2,1)S(1)}, u32[]{:S(2)}, u32[]{:S(2)}) %collective-permute-start.6) | collective-permute-done | bytes 393248 | tf_op jit(solution)/shard_map/ppermute | solution.py:22
  75.3 0.7 slice_bitcast_fusion.3
  76.0 0.7 slice_bitcast_fusion.2
  76.7 3.2 %collective-permute-start.9 = (bf16[96,1024]{1,0:T(8,128)(2,1)}, bf16[96,1024]{1,0:T(8,128)(2,1)}, u32[]{:S(2)}, u32[]{:S(2)}) collective-permute-start(bf16[96,1024]{1,0:T(8,128)(2,1)} %slice_bitcast_fusion.2), channel_id=1, source_target_pairs={{0,12},{1,13},{2,14},{3,15},{4,0},{5,1},{6,2},{7,3},{8,4},{9,5},{1... | collective-permute-start | bytes 589832 | tf_op jit(solution)/shard_map/ppermute | solution.py:22
  80.1 0.6 reduce_max.9
  81.4 0.6 stack.107.tab
  82.1 3.0 %shard_map.51 = bf16[512,1152]{1,0:T(8,128)(2,1)} custom-call(s32[8]{0:T(128)S(1)} %stack.128.tab, s32[512,1]{1,0:T(8,128)S(1)} %get-tuple-element.537.slot, bf16[96,1152]{1,0:T(8,128)(2,1)S(1)} %copy-done.1, bf16[96,1152]{1,0:T(8,128)(2,1)S(1)} %collective-permute-done.10.s1, bf16[2,96,1152]{2,1,0:T(8,128)(2,1)S(1)} %collective-permute-done.11.s2, ...), custom_call_target="tpu_custom_call" | custom-call | flops 905969664 | bytes 2359296 | tf_op jit(solution)/shard_map/pallas_call | solution.py:261
  85.1 2.2 %shard_map.50 = bf16[512,1024]{1,0:T(8,128)(2,1)S(1)} custom-call(s32[8]{0:T(128)S(1)} %stack.116.tab, s32[512,1]{1,0:T(8,128)S(1)} %get-tuple-element.537.slot, bf16[96,1024]{1,0:T(8,128)(2,1)S(1)} %collective-permute-done.4.s0, bf16[96,1024]{1,0:T(8,128)(2,1)S(1)} %collective-permute-done.5.s1, bf16[2,96,1024]{2,1,0:T(8,128)(2,1)S(1)} %collective-permute-done.6.s2, ...), custom_call_target="tpu_custom_call" | custom-call | flops 805306368 | bytes 2097152 | tf_op jit(solution)/shard_map/pallas_call | solution.py:261
  87.2 1.3 %copy.10 = bf16[512,1024]{0,1:T(8,128)(2,1)} copy(bf16[512,1024]{1,0:T(8,128)(2,1)S(1)} %shard_map.50) | data formatting | bytes 2097152 | tf_op jit(solution)/shard_map/while | solution.py:422
  88.6 1.5 %copy.12.mine = bf16[512,1024]{1,0:T(8,128)(2,1)S(1)} copy(bf16[512,1024]{0,1:T(8,128)(2,1)} %get-tuple-element.1059) | data formatting | bytes 2097152 | tf_op jit(solution)/shard_map/while | solution.py:422
  90.4 13.5 %inverse.1.inv = f32[512,512]{1,0:T(8,128)S(1)} custom-call(f32[128,4,512]{2,1,0:T(4,128)} %get-tuple-element.1058), custom_call_target="tpu_custom_call" | custom-call | flops 11274289152 | bytes 2097152 | tf_op jit(solution)/shard_map/inverse/pallas_call | solution.py:234
  103.9 1.0 copy-done
  104.9 1.0 copy-done.5
  105.9 10.1 %finish.1 = (f32[2048,1024]{1,0:T(8,128)}, bf16[128,2048]{1,0:T(8,128)(2,1)}) custom-call(s32[8]{0:T(128)} %stack.107.tab, s32[1,512]{1,0:T(1,128)S(1)} %get-tuple-element.1061, f32[512,512]{1,0:T(8,128)} %copy-done, bf16[512,1152]{1,0:T(8,128)(2,1)S(1)} %copy-done.4, bf16[512,1024]{1,0:T(8,128)(2,1)} %copy-done.3, bf16[512,1024]{1,0:T(8,128)(2,1)} %copy-done.5, ...), custom_call_target="tpu_custom_call" | custom-call | flops 2147483648 | bytes 16777216 | tf_op jit(solution)/shard_map/finish/pallas_call | solution.py:319
  (31 shorter events, 0.7 us)
Async XLA Ops:
  7.0 13.8 %collective-permute-start.10 = (bf16[96,1152]{1,0:T(8,128)(2,1)}, bf16[96,1152]{1,0:T(8,128)(2,1)S(1)}, u32[]{:S(2)}, u32[]{:S(2)}) collective-permute-start(bf16[96,1152]{1,0:T(8,128)(2,1)} %get-tuple-element.539.s0), channel_id=1, source_target_pairs={{0,64},{16,80},{32,96},{48,112},{64,0},{80,16},{96,32},{112,48},{1... | collective-permute-start | bytes 663560 | tf_op jit(solution)/shard_map/ppermute | solution.py:22
  11.5 23.5 %collective-permute-start.4 = (bf16[96,1024]{1,0:T(8,128)(2,1)}, bf16[96,1024]{1,0:T(8,128)(2,1)S(1)}, u32[]{:S(2)}, u32[]{:S(2)}) collective-permute-start(bf16[96,1024]{1,0:T(8,128)(2,1)} %get-tuple-element.538), channel_id=1, source_target_pairs={{0,0},{1,1},{2,18},{3,19},{4,36},{5,37},{6,54},{7,55},{8,72},{9,73... | collective-permute-start | bytes 589832 | tf_op jit(solution)/shard_map/ppermute | solution.py:395
  22.5 34.6 %collective-permute-start.11 = (bf16[2,96,1152]{2,1,0:T(8,128)(2,1)}, bf16[2,96,1152]{2,1,0:T(8,128)(2,1)S(1)}, u32[]{:S(2)}, u32[]{:S(2)}) collective-permute-start(bf16[2,96,1152]{2,1,0:T(8,128)(2,1)} %pad_maximum_fusion.1), channel_id=1, source_target_pairs={{0,16},{16,32},{32,48},{48,0},{64,80},{80,96},{96,112},{112,64},{1... | collective-permute-start | bytes 1327112 | tf_op jit(solution)/shard_map/ppermute | solution.py:22
  22.5 22.7 %all-to-all-start = ((f32[128,4,128]{2,1,0:T(4,128)}), f32[128,4,128]{2,1,0:T(4,128)S(1)}, u32[]{:S(2)}, u32[]{:S(2)}) async-start(f32[128,4,128]{2,1,0:T(4,128)} %get-tuple-element.535), calls=%async_computation | async-start | bytes 524288 | tf_op jit(solution)/shard_map/all_to_all | solution.py:388
  35.1 18.7 %collective-permute-start.5 = (bf16[96,1024]{1,0:T(8,128)(2,1)S(1)}, bf16[96,1024]{1,0:T(8,128)(2,1)S(1)}, u32[]{:S(2)}, u32[]{:S(2)}) collective-permute-start(bf16[96,1024]{1,0:T(8,128)(2,1)S(1)} %collective-permute-done.4.s0), channel_id=1, source_target_pairs={{0,2},{1,3},{2,0},{3,1},{4,6},{5,7},{6,4},{7,5},{8,10},{9,11},{10,... | collective-permute-start | bytes 589832 | tf_op jit(solution)/shard_map/ppermute | solution.py:22
  36.9 21.7 %collective-permute-start.12 = (bf16[2,96,1152]{2,1,0:T(8,128)(2,1)}, bf16[2,96,1152]{2,1,0:T(8,128)(2,1)S(1)}, u32[]{:S(2)}, u32[]{:S(2)}) collective-permute-start(bf16[2,96,1152]{2,1,0:T(8,128)(2,1)} %pad_maximum_fusion.1), channel_id=1, source_target_pairs={{0,48},{16,0},{32,16},{48,32},{64,112},{80,64},{96,80},{112,96},{1... | collective-permute-start | bytes 1327112 | tf_op jit(solution)/shard_map/ppermute | solution.py:22
  47.9 34.2 %copy-start.1 = (bf16[96,1152]{1,0:T(8,128)(2,1)S(1)}, bf16[96,1152]{1,0:T(8,128)(2,1)}, u32[]{:S(2)}) copy-start(bf16[96,1152]{1,0:T(8,128)(2,1)} %get-tuple-element.539.s0) | copy-start | bytes 663556
  47.9 40.7 %all-to-all-start.1 = ((f32[128,4,512]{2,1,0:T(4,128)}), f32[128,4,512]{2,1,0:T(4,128)}, u32[]{:S(2)}, u32[]{:S(2)}) async-start(f32[128,4,512]{2,1,0:T(4,128)} %get-tuple-element.536), calls=%async_computation.1 | async-start | bytes 2097152 | tf_op jit(solution)/shard_map/all_to_all | solution.py:398
  53.8 21.5 %collective-permute-start.6 = (bf16[2,96,1024]{2,1,0:T(8,128)(2,1)S(1)}, bf16[2,96,1024]{2,1,0:T(8,128)(2,1)S(1)}, u32[]{:S(2)}, u32[]{:S(2)}) collective-permute-start(bf16[2,96,1024]{2,1,0:T(8,128)(2,1)S(1)} %pad_maximum_fusion.2), channel_id=1, source_target_pairs={{0,4},{1,5},{2,6},{3,7},{4,8},{5,9},{6,10},{7,11},{8,12},{9,13},{1... | collective-permute-start | bytes 1179656 | tf_op jit(solution)/shard_map/ppermute | solution.py:22
  54.7 21.3 %collective-permute-start.7 = (bf16[2,96,1024]{2,1,0:T(8,128)(2,1)S(1)}, bf16[2,96,1024]{2,1,0:T(8,128)(2,1)S(1)}, u32[]{:S(2)}, u32[]{:S(2)}) collective-permute-start(bf16[2,96,1024]{2,1,0:T(8,128)(2,1)S(1)} %pad_maximum_fusion.2), channel_id=1, source_target_pairs={{0,12},{1,13},{2,14},{3,15},{4,0},{5,1},{6,2},{7,3},{8,4},{9,5},{1... | collective-permute-start | bytes 1179656 | tf_op jit(solution)/shard_map/ppermute | solution.py:22
  57.8 24.2 %collective-permute-start.13 = (bf16[96,1152]{1,0:T(8,128)(2,1)}, bf16[96,1152]{1,0:T(8,128)(2,1)S(1)}, u32[]{:S(2)}, u32[]{:S(2)}) collective-permute-start(bf16[96,1152]{1,0:T(8,128)(2,1)} %slice_bitcast_fusion.1), channel_id=1, source_target_pairs={{0,16},{16,32},{32,48},{48,0},{64,80},{80,96},{96,112},{112,64},{1... | collective-permute-start | bytes 663560 | tf_op jit(solution)/shard_map/ppermute | solution.py:22
  59.4 22.7 %collective-permute-start.14 = (bf16[96,1152]{1,0:T(8,128)(2,1)}, bf16[96,1152]{1,0:T(8,128)(2,1)S(1)}, u32[]{:S(2)}, u32[]{:S(2)}) collective-permute-start(bf16[96,1152]{1,0:T(8,128)(2,1)} %slice_bitcast_fusion), channel_id=1, source_target_pairs={{0,48},{16,0},{32,16},{48,32},{64,112},{80,64},{96,80},{112,96},{1... | collective-permute-start | bytes 663560 | tf_op jit(solution)/shard_map/ppermute | solution.py:22
  76.0 9.0 %collective-permute-start.8 = (bf16[96,1024]{1,0:T(8,128)(2,1)}, bf16[96,1024]{1,0:T(8,128)(2,1)}, u32[]{:S(2)}, u32[]{:S(2)}) collective-permute-start(bf16[96,1024]{1,0:T(8,128)(2,1)} %slice_bitcast_fusion.3), channel_id=1, source_target_pairs={{0,4},{1,5},{2,6},{3,7},{4,8},{5,9},{6,10},{7,11},{8,12},{9,13},{1... | collective-permute-start | bytes 589832 | tf_op jit(solution)/shard_map/ppermute | solution.py:22
  76.7 8.3 %collective-permute-start.9 = (bf16[96,1024]{1,0:T(8,128)(2,1)}, bf16[96,1024]{1,0:T(8,128)(2,1)}, u32[]{:S(2)}, u32[]{:S(2)}) collective-permute-start(bf16[96,1024]{1,0:T(8,128)(2,1)} %slice_bitcast_fusion.2), channel_id=1, source_target_pairs={{0,12},{1,13},{2,14},{3,15},{4,0},{5,1},{6,2},{7,3},{8,4},{9,5},{1... | collective-permute-start | bytes 589832 | tf_op jit(solution)/shard_map/ppermute | solution.py:22
  85.0 3.5 %copy-start.6 = (s32[1,512]{1,0:T(1,128)S(1)}, s32[1,512]{1,0:T(1,128)}, u32[]{:S(2)}) copy-start(s32[1,512]{1,0:T(1,128)} %index.3) | copy-start | bytes 6148
  90.1 13.8 %copy-start.3 = (bf16[512,1024]{1,0:T(8,128)(2,1)}, bf16[512,1024]{1,0:T(8,128)(2,1)S(1)}, u32[]{:S(2)}) copy-start(bf16[512,1024]{1,0:T(8,128)(2,1)S(1)} %copy.12.mine) | copy-start | bytes 3145732
  90.1 14.8 %collective-permute-start.15 = (bf16[512,1024]{1,0:T(8,128)(2,1)S(1)}, bf16[512,1024]{1,0:T(8,128)(2,1)S(1)}, u32[]{:S(2)}, u32[]{:S(2)}) collective-permute-start(bf16[512,1024]{1,0:T(8,128)(2,1)S(1)} %copy.12.mine), channel_id=1, source_target_pairs={{0,1},{1,0},{2,3},{3,2},{4,5},{5,4},{6,7},{7,6},{8,9},{9,8},{10,11... | collective-permute-start | bytes 3145736 | tf_op jit(solution)/shard_map/ppermute | solution.py:22
  90.4 15.5 %copy-start.2 = (bf16[128,2048]{1,0:T(8,128)(2,1)S(1)}, bf16[128,2048]{1,0:T(8,128)(2,1)}, u32[]{:S(2)}) copy-start(bf16[128,2048]{1,0:T(8,128)(2,1)} %get-tuple-element.1064) | copy-start | bytes 1572868
  90.4 15.5 %copy-start.4 = (bf16[512,1152]{1,0:T(8,128)(2,1)S(1)}, bf16[512,1152]{1,0:T(8,128)(2,1)}, u32[]{:S(2)}) copy-start(bf16[512,1152]{1,0:T(8,128)(2,1)} %get-tuple-element.1060) | copy-start | bytes 3538948
  103.9 1.0 copy-start
  104.9 1.0 copy-start.5
